TPU v7x, 32 devices: a whole 2x2x4 slice. The times are simulated.
32 devices in a mesh: tm: 8 (over z, x), state: 4 (over y, core).
Axes of the slice: x: 2, y: 2, z: 4, core: 2. Of those that a mesh axis runs over, the one named last changes fastest.
Arguments:
- dyn_cols: int32 [256, 8, 3], P('tm', 'state'), may hold values from 0 to 7, as said below
- dyn_vals: bfloat16 [256, 8, 64, 192], P('tm', 'state'), may hold values from -1 to 1
- obs_blocks: int32 [256, 2], P('tm'), may hold values from 0 to 7
- obs_op: bfloat16 [256, 64, 128], P('tm'), may hold values from -0.75 to 0.75
- obs_counts: int32 [256], P('tm'), may hold values from 32 to 128, as said below
- obs_values: float32 [256, 128], P('tm'), may hold values from -6 to 6
- gain: bfloat16 [256, 512, 128], P('tm', 'state'), may hold values from -0.0078125 to 0.0078125
- sources: float32 [256, 512], P('tm', 'state'), may hold values from -0.625 to 0.625
- prior: float32 [512], replicated, may hold values from -6 to 6
Outputs:
- filtered: float32 [256, 512], P('tm', 'state')
Inputs may be any that keep to these rules, and one draw needn't show every extreme that they name: `dyn_cols`: for every step and block row i, the first entry is i itself and the 3 entries are distinct block columns. `obs_counts`: some step has all 128 observations present.
All inputs are finite; a program needn't handle non-finite values.
Results may differ from a plain program's by a relative error of at most 0.0003.
The roundings to bfloat16 on the way count: a program that leaves them out, or rounds other values in their place, can miss the bound.
Values may be sent and summed in bfloat16 or wider, within the bound.
No kernel may reach another device: no remote copies, remote signals or barrier semaphores. Data moves between devices by JAX's collectives and lax.ppermute only.
A program may use at most 128 MiB of HBM per device.

v0:
```python
import jax
import jax.numpy as jnp
from jax import lax
from jax.sharding import PartitionSpec as P

NS = 512
BS = 64
KF = 3
OBS = 128
NB = 8
OB = 2
HIGHEST = lax.Precision.HIGHEST


def shifted(shard, axis, by):
    devices = lax.axis_size(axis)
    pairs = [(i, i + by) for i in range(devices) if 0 <= i + by < devices]
    return lax.ppermute(shard, axis, pairs)


def split_product(matrix, operand):
    leading = operand.astype(jnp.bfloat16)
    remainder = (operand - lax.optimization_barrier(leading).astype(jnp.float32)).astype(
        jnp.bfloat16
    )
    return jnp.dot(matrix, leading, preferred_element_type=jnp.float32) + jnp.dot(
        matrix, remainder, preferred_element_type=jnp.float32
    )


def body(dyn_cols, dyn_vals, obs_blocks, obs_op, obs_counts, obs_values, gain, sources, prior):
    step_count = dyn_vals.shape[0]
    local_blocks = dyn_vals.shape[1]
    local_rows = local_blocks * BS
    state_index = lax.axis_index("state")
    time_index = lax.axis_index("tm")
    onehot = (dyn_cols[..., None] == jnp.arange(NB)).astype(jnp.bfloat16)
    blocks = dyn_vals.reshape(step_count, local_blocks, BS, KF, BS)
    forward = jnp.einsum("tikc,tiakb->tiacb", onehot, blocks, preferred_element_type=jnp.float32)
    forward = forward.reshape(step_count, local_blocks, BS, NS)
    forward_narrow = forward.astype(jnp.bfloat16)
    owned = state_index * local_blocks + jnp.arange(local_blocks)
    select = obs_blocks[:, :, None] == owned[None, None, :]
    selected = jnp.einsum(
        "tos,tsbn->tobn",
        select.astype(jnp.bfloat16),
        forward_narrow,
        preferred_element_type=jnp.float32,
    ).astype(jnp.bfloat16)
    operator_blocks = obs_op.reshape(step_count, BS, OB, BS)
    image_part = jnp.einsum(
        "tboa,tobn->toan", operator_blocks, selected, preferred_element_type=jnp.float32
    )
    image_part = image_part.reshape(step_count, OBS, NS)
    source_sel = jnp.einsum(
        "tos,tsb->tob",
        select.astype(jnp.float32),
        sources.reshape(step_count, local_blocks, BS),
        precision=HIGHEST,
    )
    source_part = jnp.einsum(
        "tboa,tob->toa", operator_blocks.astype(jnp.float32), source_sel, precision=HIGHEST
    )
    source_part = source_part.reshape(step_count, OBS)
    image_sum, source_sum = (
        lax.psum(image_part.astype(jnp.bfloat16), "state").astype(jnp.float32),
        lax.psum(source_part.astype(jnp.bfloat16), "state").astype(jnp.float32),
    )
    active = jnp.arange(OBS)[None, :] < obs_counts[:, None]
    masked = jnp.where(
        active[:, :, None], image_sum.astype(jnp.bfloat16), jnp.zeros((), jnp.bfloat16)
    )
    source_image = lax.optimization_barrier(source_sum.astype(jnp.bfloat16)).astype(jnp.float32)
    innovation = jnp.where(active, obs_values - source_image, 0.0)
    correction = jnp.einsum("tro,ton->trn", gain, masked, preferred_element_type=jnp.float32)
    element = (forward.reshape(step_count, local_rows, NS) - correction).astype(jnp.bfloat16)
    offset = sources + jnp.einsum(
        "tro,to->tr", gain.astype(jnp.float32), innovation, precision=HIGHEST
    )
    full_elements = lax.all_gather(element, "state", axis=1, tiled=True)
    full_offsets = lax.all_gather(offset, "state", axis=1, tiled=True)
    start_cols = (
        jnp.arange(NS)[:, None] == (state_index * local_rows + jnp.arange(local_rows))[None, :]
    ).astype(jnp.float32)

    def compose(carry, inputs):
        product, vector = carry
        matrix, shift_term = inputs
        product = split_product(matrix, product)
        vector = split_product(matrix, vector) + shift_term
        return ((product, vector), None)

    (column_product, span_offset), _ = lax.scan(
        compose, (start_cols, jnp.zeros((NS,), jnp.float32)), (full_elements, full_offsets)
    )
    span_matrix = lax.all_gather(column_product, "state", axis=1, tiled=True)
    first_span = time_index == 0

    def hand_over(turn, current):
        leaving = jnp.dot(span_matrix, current, precision=HIGHEST) + span_offset
        arriving = shifted(leaving, "tm", 1)
        return jnp.where(first_span, prior, arriving)

    entry = lax.fori_loop(0, lax.axis_size("tm") - 1, hand_over, prior)

    def sweep(current, inputs):
        matrix, shift_term = inputs
        new_mean = split_product(matrix, current) + shift_term
        return (new_mean, lax.dynamic_slice_in_dim(new_mean, state_index * local_rows, local_rows))

    _, filtered = lax.scan(sweep, entry, (full_elements, full_offsets))
    return filtered


def solution(mesh):
    return jax.shard_map(
        body,
        mesh=mesh,
        in_specs=(
            P("tm", "state", None),
            P("tm", "state", None, None),
            P("tm", None),
            P("tm", None, None),
            P("tm"),
            P("tm", None),
            P("tm", "state", None),
            P("tm", "state"),
            P(),
        ),
        out_specs=P("tm", "state"),
        check_vma=False,
    )
```

profile of v0, /device:TPU:8, one launch (start us, length us, event | category | flops | bytes accessed | tf_op | source)
XLA Modules:
  0.0 674.5 jit_solution(3673502673892375149)
XLA Ops:
  8.2 2.4 reshape.47
  10.6 4.5 copy.18
  15.1 7.1 %copy.19 = bf16[32,2,64,3,64]{4,3,2,1,0:T(4,128)(2,1)} copy(bf16[32,2,64,3,64]{2,4,3,1,0:T(8,128)(2,1)} %bitcast.140) | data formatting | bytes 3145728 | tf_op jit(solution)/shard_map/reshape | solution.py:38
  22.3 10.6 %fusion.48 = (bf16[32,2,64,8,64]{4,3,2,1,0:T(8,128)(2,1)}, f32[32,2,64,8,64]{4,3,2,1,0:T(8,128)}) fusion(bf16[32,2,64,3,64]{4,3,2,1,0:T(4,128)(2,1)} %copy.19, s32[32,2,3]{2,1,0:T(2,128)S(1)} %copy.17), kind=kOutput, calls=%fused_computation.66 | convolution fusion | flops 14681600 | bytes 14156544 | tf_op jit(solution)/shard_map/tikc,tiakb->tiacb/dot_general | solution.py:39
  32.9 11.8 %convert_element_type.77 = bf16[32,2,64,512]{3,2,1,0:T(8,128)(2,1)} reshape(bf16[32,2,64,8,64]{4,3,2,1,0:T(8,128)(2,1)} %get-tuple-element.218) | data formatting | bytes 8388608 | tf_op jit(solution)/shard_map/convert_element_type | solution.py:41
  44.7 8.7 %fusion.28 = bf16[32,2,64,512]{3,1,2,0:T(2,128)(2,1)S(1)} fusion(bf16[32,2,64,512]{3,2,1,0:T(8,128)(2,1)} %convert_element_type.77, s32[2]{0:T(128)S(1)} %iota_add_fusion, s32[32,2]{1,0:T(8,128)S(1)} %copy.20), kind=kOutput, calls=%fused_computation.42 | convolution fusion | flops 8388736 | bytes 8388872 | tf_op jit(solution)/shard_map/tos,tsbn->tobn/dot_general | solution.py:44
  53.5 3.2 fusion.32
  56.7 6.5 copy.22
  63.2 14.5 %reshape_reshape.3 = f32[32,128,512]{2,1,0:T(8,128)} reshape(f32[32,2,64,8,64]{4,3,2,1,0:T(8,128)} %get-tuple-element.219) | data formatting | bytes 16777216 | tf_op jit(solution)/shard_map/reshape;reshape | solution.py:76
  77.7 9.0 %copy.23 = f32[32,128,512]{1,2,0:T(8,128)} copy(f32[32,128,512]{2,1,0:T(8,128)} %reshape_reshape.3) | data formatting | bytes 16777216 | tf_op jit(solution)/shard_map/reshape;reshape | solution.py:76
  86.8 63.2 %all-reduce.2.cloned.1.call-done = bf16[32,128,512]{1,2,0:T(8,128)(2,1)} async-done(((bf16[32,128,512]{1,2,0:T(8,128)(2,1)}), bf16[32,128,512]{1,2,0:T(8,128)(2,1)}) %all-reduce.2.cloned.1.call-update) | async-done | bytes 4194320 | tf_op jit(solution)/shard_map/psum | solution.py:66
  150.0 7.9 %fusion.23 = bf16[32,128,512]{1,2,0:T(8,128)(2,1)} fusion(f32[32,128,512]{1,2,0:T(8,128)} %copy.23, bf16[32,128,128]{2,1,0:T(8,128)(2,1)S(1)} %copy-done, bf16[32,128,512]{1,2,0:T(8,128)(2,1)} %all-reduce.2.cloned.1.call-done, pred[32,128]{1,0:T(8,128)(4,1)S(1)} %iota_compare_fusion.2), kind=kOutput, calls=%fused_computation.36 | convolution fusion | flops 543162368 | bytes 17829888 | tf_op jit(solution)/shard_map/tro,ton->trn/dot_general | solution.py:75
  160.0 6.4 psum.15
  168.3 5.5 all_gather.10
  173.8 92.7 %all-gather.3.cloned.1.call-done = bf16[32,512,512]{1,2,0:T(8,128)(2,1)} async-done(((bf16[32,128,512]{1,2,0:T(8,128)(2,1)}), bf16[32,512,512]{1,2,0:T(8,128)(2,1)}) %all-gather.3.cloned.1.call-update) | async-done | bytes 16777232 | tf_op jit(solution)/shard_map/all_gather | solution.py:80
  266.5 22.5 %copy.24 = bf16[32,512,512]{2,1,0:T(8,128)(2,1)} copy(bf16[32,512,512]{1,2,0:T(8,128)(2,1)} %all-gather.3.cloned.1.call-done) | data formatting | bytes 33554432
  289.1 173.2 %while.42 = (s32[]{:T(128)}, f32[512,128]{1,0:T(8,128)S(1)}, f32[512]{0:T(512)S(1)}, bf16[32,512,512]{2,1,0:T(8,128)(2,1)}, f32[32,512]{1,0:T(8,128)S(1)}) while((s32[]{:T(128)}, f32[512,128]{1,0:T(8,128)S(1)}, f32[512]{0:T(512)S(1)}, bf16[32,512,512]{2,1,0:T(8,128)(2,1)}, f32[32,512]{1,0:T(8,128)S(1)}) %tuple.69), condition=%wide.region_3.4_spmd.clone.clone, body=%wide.region_2.3_spmd.clone.sunk.clone | while | flops 135597568 | bytes 4355172 | solution.py:93
  463.1 16.9 %all-gather.5.cloned.1.call-done = f32[512,512]{1,0:T(8,128)} async-done(((f32[512,128]{1,0:T(8,128)}), f32[512,512]{1,0:T(8,128)}) %all-gather.5.cloned.1.call-update) | async-done | bytes 1048592 | tf_op jit(solution)/shard_map/all_gather | solution.py:96
  480.0 60.1 %while.40 = (s32[]{:T(128)}, f32[512]{0:T(512)S(1)}, pred[]{:T(512)}, f32[512,512]{1,0:T(8,128)}, f32[512]{0:T(512)S(1)}, /*index=5*/f32[512]{0:T(512)S(1)}) while((s32[]{:T(128)}, f32[512]{0:T(512)S(1)}, pred[]{:T(512)}, f32[512,512]{1,0:T(8,128)}, f32[512]{0:T(512)S(1)}, /*index=5*/f32[512]{0:T(512)S(1)}) %tuple.86), condition=%wide.region_5.6_spmd.clone, body=%wide.region_4.5_spmd.sunk.clone | while | flops 3146754 | bytes 1073262 | solution.py:104
  482.2 3.4 collective-permute-start
  485.6 3.0 collective-permute-done
  490.8 2.5 collective-permute-start
  493.3 3.9 collective-permute-done
  497.2 2.2 fusion.104
  501.3 4.4 collective-permute-done
  505.8 2.2 fusion.104
  509.9 4.4 collective-permute-done
  514.4 2.2 fusion.104
  518.5 4.4 collective-permute-done
  527.1 4.4 collective-permute-done
  535.7 4.4 collective-permute-done
  540.2 127.8 %while.41 = (s32[]{:T(128)}, f32[512]{0:T(512)S(1)}, f32[32,128]{1,0:T(8,128)}, bf16[32,512,512]{2,1,0:T(8,128)(2,1)}, f32[32,512]{1,0:T(8,128)S(1)}, /*index=5*/s32[]{:T(128)}) while((s32[]{:T(128)}, f32[512]{0:T(512)S(1)}, f32[32,128]{1,0:T(8,128)}, bf16[32,512,512]{2,1,0:T(8,128)(2,1)}, f32[32,512]{1,0:T(8,128)S(1)}, ...), condition=%wide.region_7.8_spmd.clone, body=%wide.region_6.7_spmd.sunk.clone | while | flops 1051650 | bytes 1080417 | solution.py:111
  (762 shorter events, 323.3 us)
Async XLA Ops:
  6.5 143.4 %copy-start = (bf16[32,128,128]{2,1,0:T(8,128)(2,1)S(1)}, bf16[32,128,128]{2,1,0:T(8,128)(2,1)}, u32[]{:S(2)}) copy-start(bf16[32,128,128]{2,1,0:T(8,128)(2,1)} %param.21) | copy-start | bytes 3145732
  6.5 143.4 %all-reduce.2.cloned.1.call-start = ((), (), s32[]{:S(2)}) async-start(), calls=%async_computation | async-start | bytes 8388608 | tf_op jit(solution)/shard_map/psum | solution.py:66
  63.2 203.3 %all-gather.3.cloned.1.call-start = ((), (), s32[]{:S(2)}) async-start(), calls=%async_computation.1 | async-start | bytes 20971520 | tf_op jit(solution)/shard_map/all_gather | solution.py:80
  77.7 9.0 %copy-start.5 = (s32[32]{0:T(128)S(1)}, s32[32]{0:T(128)}, u32[]{:S(2)}) copy-start(s32[32]{0:T(128)} %param.19) | copy-start | bytes 388
  157.9 0.7 copy-start.3
  157.9 8.6 %copy-start.4 = (f32[32,128]{1,0:T(8,128)S(1)}, f32[32,128]{1,0:T(8,128)}, u32[]{:S(2)}) copy-start(f32[32,128]{1,0:T(8,128)} %param.20) | copy-start | bytes 49156
  157.9 322.1 %all-gather.5.cloned.1.call-start = ((), (), s32[]{:S(2)}) async-start(), calls=%async_computation.2 | async-start | bytes 1310720 | tf_op jit(solution)/shard_map/all_gather | solution.py:96
  289.1 174.0 %copy-start.2 = (f32[512]{0:T(512)S(1)}, f32[512]{0:T(512)}, u32[]{:S(2)}) copy-start(f32[512]{0:T(512)} %param.23) | copy-start | bytes 6148
  462.3 0.7 copy-start.1
  482.2 6.4 collective-permute-start
  490.8 6.4 collective-permute-start
  499.4 6.4 collective-permute-start
  508.0 6.4 collective-permute-start
  516.6 6.4 collective-permute-start
  525.2 6.4 collective-permute-start
  533.8 6.4 collective-permute-start
Sparse Core Ops, SparseCore 0:
  63.3 86.6 all-reduce.1
  158.0 108.4 all-gather.2
  463.2 16.8 all-gather.4
where the time goes:
time: 687 us; the launch traced here: 674 us
  matrix products  299 us (44%)
  waiting for transfers between devices  202 us (29%)
  local copies, waits for them, and re-layouts  127 us (18%)
  starting transfers between devices  15.6 us (2%)
  between operations  13.2 us (2%)
  blocking collectives  11.9 us (2%)
    dot_general x96, matrix products, split_product(): jnp.dot(matrix, leading, preferred_element_type=jnp.float32)  126 us
    dot_general x96, matrix products, split_product(): jnp.dot(matrix, remainder, preferred_element_type=jnp.float32)  125 us
    all_gather x1, waiting for transfers between devices, body(): full_elements = lax.all_gather(element, 'state', axis=1, tiled=True)  92.7 us
    psum x1, waiting for transfers between devices, body(): lax.psum(image_part.astype(jnp.bfloat16), 'state').astype(jnp.float32)  63.2 us
    dynamic_update_slice x32, local copies, waits for them, and re-layouts, body(): _, filtered = lax.scan(sweep, entry, (full_elements, full_offsets))  41.3 us
    unnamed x17, local copies, waits for them, and re-layouts  30 us
    ppermute x7, waiting for transfers between devices, shifted(): return lax.ppermute(shard, axis, pairs)  29.1 us
    another operation x2, local copies, waits for them, and re-layouts, body(): forward.reshape(step_count, local_rows, NS) - correction  23.5 us
  transfers between devices with their start and end apart: 10, of which 10 were waited for; matrix products, arithmetic and copies ran while one was open for 4% of the time, Pallas kernels for 0%

commit v1 on v0

--- a/solution.py
+++ b/solution.py
@@ -10,6 +10,12 @@
 NB = 8
 OB = 2
 HIGHEST = lax.Precision.HIGHEST
+windows_assign = lambda sheet: jnp.concatenate(
+    lax.all_to_all(
+        jnp.stack([sheet] * lax.axis_size("state"), axis=0), "state", split_axis=0, concat_axis=0
+    ),
+    axis=1,
+)
 
 
 def shifted(shard, axis, by):
@@ -77,7 +83,7 @@
     offset = sources + jnp.einsum(
         "tro,to->tr", gain.astype(jnp.float32), innovation, precision=HIGHEST
     )
-    full_elements = lax.all_gather(element, "state", axis=1, tiled=True)
+    full_elements = windows_assign(element)
     full_offsets = lax.all_gather(offset, "state", axis=1, tiled=True)
     start_cols = (
         jnp.arange(NS)[:, None] == (state_index * local_rows + jnp.arange(local_rows))[None, :]

time: 687 us -> 784 us (1.14)
  blocking collectives: 11.9 us -> 188 us
  waiting for transfers between devices: 202 us -> 110 us
    psum x1, blocking collectives: 6.43 us -> 183 us  [body(): lax.psum(source_part.astype(jnp.bfloat16), 'state').astype(jnp.float32)]
    all_gather x1 -> x0, waiting for transfers between devices: 92.7 us -> none  [body(): full_elements = lax.all_gather(element, 'state', axis=1, tiled=True)]
    unnamed x17 -> x16, local copies, waits for them, and re-layouts: 30 us -> 6.85 us
    all_to_all x0 -> x1, local copies, waits for them, and re-layouts: none -> 13.9 us  [lax.all_to_all(jnp.stack([sheet] * lax.axis_size('state'), axis=0), 'stat...]
  transfers between devices with their start and end apart: 10 -> 10, of which waited for: 10 -> 9; matrix products, arithmetic and copies ran while one was open for 4% -> 3% of each run, Pallas kernels for 0% -> 0%
where the time goes in v1:
time: 784 us; the launch traced here: 771 us
  matrix products  299 us (38%)
  blocking collectives  188 us (24%)
  local copies, waits for them, and re-layouts  132 us (17%)
  waiting for transfers between devices  110 us (14%)
  starting transfers between devices  22.8 us (3%)
  between operations  13.6 us (2%)
    psum x1, blocking collectives, body(): lax.psum(source_part.astype(jnp.bfloat16), 'state').astype(jnp.float32)  183 us
    dot_general x96, matrix products, split_product(): jnp.dot(matrix, leading, preferred_element_type=jnp.float32)  126 us
    dot_general x96, matrix products, split_product(): jnp.dot(matrix, remainder, preferred_element_type=jnp.float32)  125 us
    psum x1, waiting for transfers between devices, body(): lax.psum(image_part.astype(jnp.bfloat16), 'state').astype(jnp.float32)  63.2 us
    dynamic_update_slice x32, local copies, waits for them, and re-layouts, body(): _, filtered = lax.scan(sweep, entry, (full_elements, full_offsets))  41.3 us
    ppermute x7, waiting for transfers between devices, shifted(): return lax.ppermute(shard, axis, pairs)  29.1 us
    another operation x2, local copies, waits for them, and re-layouts, body(): forward.reshape(step_count, local_rows, NS) - correction  23.5 us
    all_gather x1, waiting for transfers between devices, body(): span_matrix = lax.all_gather(column_product, 'state', axis=1, tiled=True)  18 us
  transfers between devices with their start and end apart: 10, of which 9 were waited for; matrix products, arithmetic and copies ran while one was open for 3% of the time, Pallas kernels for 0%

profile of v1, /device:TPU:8, one launch (start us, length us, event | category | flops | bytes accessed | tf_op | source)
XLA Modules:
  0.0 771.2 jit_solution(16532251579400438252)
XLA Ops:
  8.2 2.4 reshape.55
  10.6 4.5 copy.35
  15.1 7.1 copy.36
  22.3 10.6 %fusion.50 = (bf16[32,2,64,8,64]{4,3,2,1,0:T(8,128)(2,1)}, f32[32,2,64,8,64]{4,3,2,1,0:T(8,128)}) fusion(bf16[32,2,64,3,64]{4,3,2,1,0:T(4,128)(2,1)} %copy.36, s32[32,2,3]{2,1,0:T(2,128)S(1)} %copy.34), kind=kOutput, calls=%fused_computation.66 | convolution fusion | flops 14681600 | bytes 14156544 | tf_op jit(solution)/shard_map/tikc,tiakb->tiacb/dot_general | solution.py:45
  32.9 11.8 %convert_element_type.77 = bf16[32,2,64,512]{3,2,1,0:T(8,128)(2,1)} reshape(bf16[32,2,64,8,64]{4,3,2,1,0:T(8,128)(2,1)} %get-tuple-element.196) | data formatting | bytes 8388608 | tf_op jit(solution)/shard_map/convert_element_type | solution.py:47
  44.7 8.7 %convolution_convert_fusion = bf16[32,2,64,512]{3,1,2,0:T(2,128)(2,1)S(1)} fusion(bf16[32,2,64,512]{3,2,1,0:T(8,128)(2,1)} %convert_element_type.77, s32[2]{0:T(128)S(1)} %iota_add_fusion, s32[32,2]{1,0:T(8,128)S(1)} %copy.37), kind=kOutput, calls=%fused_computation.37 | convolution fusion | flops 10485888 | bytes 8388872 | tf_op jit(solution)/shard_map/tos,tsbn->tobn/dot_general | solution.py:50
  53.4 3.2 fusion.32
  56.7 6.4 copy.41
  63.1 14.5 %reshape_reshape.3 = f32[32,128,512]{2,1,0:T(8,128)} reshape(f32[32,2,64,8,64]{4,3,2,1,0:T(8,128)} %get-tuple-element.197) | data formatting | bytes 16777216 | tf_op jit(solution)/shard_map/reshape;reshape | solution.py:82
  77.6 9.0 %copy.42 = f32[32,128,512]{1,2,0:T(8,128)} copy(f32[32,128,512]{2,1,0:T(8,128)} %reshape_reshape.3) | data formatting | bytes 16777216 | tf_op jit(solution)/shard_map/reshape;reshape | solution.py:82
  86.7 63.2 %all-reduce.2.cloned.1.call-done = bf16[32,128,512]{1,2,0:T(8,128)(2,1)} async-done(((bf16[32,128,512]{1,2,0:T(8,128)(2,1)}), bf16[32,128,512]{1,2,0:T(8,128)(2,1)}) %all-reduce.2.cloned.1.call-update) | async-done | bytes 4194320 | tf_op jit(solution)/shard_map/psum | solution.py:72
  149.9 7.9 %fusion.23 = bf16[32,128,512]{1,2,0:T(8,128)(2,1)} fusion(f32[32,128,512]{1,2,0:T(8,128)} %copy.42, bf16[32,128,128]{2,1,0:T(8,128)(2,1)S(1)} %copy-done, bf16[32,128,512]{1,2,0:T(8,128)(2,1)} %all-reduce.2.cloned.1.call-done, pred[32,128]{1,0:T(8,128)(4,1)S(1)} %iota_compare_fusion.2), kind=kOutput, calls=%fused_computation.36 | convolution fusion | flops 543162368 | bytes 17829888 | tf_op jit(solution)/shard_map/tro,ton->trn/dot_general | solution.py:81
  157.8 6.5 copy.43
  164.3 7.4 stack.2
  171.7 7.1 all-to-all-start
  180.5 182.9 %psum.15 = bf16[32,128]{1,0:T(8,128)(2,1)S(1)} all-reduce(bf16[32,128]{1,0:T(8,128)(2,1)S(1)} %convert_element_type.84), channel_id=1, replica_groups=mesh['tm'=8,'state'=4] {'state'}, use_global_device_ids=true, to_apply=%region_1.0 | all-reduce | flops 4096 | bytes 16384 | tf_op jit(solution)/shard_map/psum | solution.py:73
  365.2 5.2 all_gather.6
  370.5 13.9 %copy.44 = bf16[4,32,128,512]{3,2,0,1:T(8,128)(2,1)} copy(bf16[4,32,128,512]{3,2,1,0:T(8,128)(2,1)} %all-to-all-done) | data formatting | bytes 33554432 | tf_op jit(solution)/shard_map/all_to_all | solution.py:14
  384.4 173.2 %while.42 = (s32[]{:T(128)}, f32[512,128]{1,0:T(8,128)S(1)}, f32[512]{0:T(512)S(1)}, bf16[32,512,512]{2,1,0:T(8,128)(2,1)}, f32[32,512]{1,0:T(8,128)S(1)}) while((s32[]{:T(128)}, f32[512,128]{1,0:T(8,128)S(1)}, f32[512]{0:T(512)S(1)}, bf16[32,512,512]{2,1,0:T(8,128)(2,1)}, f32[32,512]{1,0:T(8,128)S(1)}) %tuple.78), condition=%wide.region_3.4_spmd.clone.clone, body=%wide.region_2.3_spmd.clone.sunk.clone | while | flops 135597568 | bytes 4355172 | solution.py:99
  558.4 18.0 %all-gather.2.cloned.1.call-done = f32[512,512]{1,0:T(8,128)} async-done(((f32[512,128]{1,0:T(8,128)}), f32[512,512]{1,0:T(8,128)}) %all-gather.2.cloned.1.call-update) | async-done | bytes 1048592 | tf_op jit(solution)/shard_map/all_gather | solution.py:102
  576.4 60.1 %while.40 = (s32[]{:T(128)}, f32[512]{0:T(512)S(1)}, pred[]{:T(512)}, f32[512,512]{1,0:T(8,128)}, f32[512]{0:T(512)S(1)}, /*index=5*/f32[512]{0:T(512)S(1)}) while((s32[]{:T(128)}, f32[512]{0:T(512)S(1)}, pred[]{:T(512)}, f32[512,512]{1,0:T(8,128)}, f32[512]{0:T(512)S(1)}, /*index=5*/f32[512]{0:T(512)S(1)}) %tuple.81), condition=%wide.region_5.6_spmd.clone, body=%wide.region_4.5_spmd.sunk.clone | while | flops 3146754 | bytes 1073262 | solution.py:110
  578.6 3.4 collective-permute-start
  582.0 3.0 collective-permute-done
  585.0 2.2 fusion.106
  587.2 2.5 collective-permute-start
  589.7 3.9 collective-permute-done
  597.7 4.4 collective-permute-done
  606.3 4.4 collective-permute-done
  614.9 4.4 collective-permute-done
  623.5 4.4 collective-permute-done
  632.1 4.4 collective-permute-done
  636.6 127.8 %while.41 = (s32[]{:T(128)}, f32[512]{0:T(512)S(1)}, f32[32,128]{1,0:T(8,128)}, bf16[32,512,512]{2,1,0:T(8,128)(2,1)}, f32[32,512]{1,0:T(8,128)S(1)}, /*index=5*/s32[]{:T(128)}) while((s32[]{:T(128)}, f32[512]{0:T(512)S(1)}, f32[32,128]{1,0:T(8,128)}, bf16[32,512,512]{2,1,0:T(8,128)(2,1)}, f32[32,512]{1,0:T(8,128)S(1)}, ...), condition=%wide.region_7.8_spmd.clone, body=%wide.region_6.7_spmd.sunk.clone | while | flops 1051650 | bytes 1080417 | solution.py:117
  (763 shorter events, 327.1 us)
Async XLA Ops:
  6.5 143.4 %copy-start = (bf16[32,128,128]{2,1,0:T(8,128)(2,1)S(1)}, bf16[32,128,128]{2,1,0:T(8,128)(2,1)}, u32[]{:S(2)}) copy-start(bf16[32,128,128]{2,1,0:T(8,128)(2,1)} %param.21) | copy-start | bytes 3145732
  6.5 143.4 %all-reduce.2.cloned.1.call-start = ((), (), s32[]{:S(2)}) async-start(), calls=%async_computation.1 | async-start | bytes 8388608 | tf_op jit(solution)/shard_map/psum | solution.py:72
  77.6 9.0 %copy-start.5 = (s32[32]{0:T(128)S(1)}, s32[32]{0:T(128)}, u32[]{:S(2)}) copy-start(s32[32]{0:T(128)} %param.19) | copy-start | bytes 388
  171.7 7.4 copy-start.3
  171.7 191.7 %copy-start.4 = (f32[32,128]{1,0:T(8,128)S(1)}, f32[32,128]{1,0:T(8,128)}, u32[]{:S(2)}) copy-start(f32[32,128]{1,0:T(8,128)} %param.20) | copy-start | bytes 49156
  171.7 198.8 %all-to-all-start = ((bf16[4,32,128,512]{3,2,1,0:T(8,128)(2,1)}), bf16[4,32,128,512]{3,2,1,0:T(8,128)(2,1)}, u32[]{:S(2)}, u32[]{:S(2)}) async-start(bf16[4,32,128,512]{3,2,1,0:T(8,128)(2,1)} %stack.2), calls=%async_computation | async-start | bytes 33554432 | tf_op jit(solution)/shard_map/all_to_all | solution.py:14
  178.8 397.6 %all-gather.2.cloned.1.call-start = ((), (), s32[]{:S(2)}) async-start(), calls=%async_computation.2 | async-start | bytes 1310720 | tf_op jit(solution)/shard_map/all_gather | solution.py:102
  384.4 174.0 %copy-start.2 = (f32[512]{0:T(512)S(1)}, f32[512]{0:T(512)}, u32[]{:S(2)}) copy-start(f32[512]{0:T(512)} %param.23) | copy-start | bytes 6148
  557.6 0.7 copy-start.1
  578.6 6.4 collective-permute-start
  587.2 6.4 collective-permute-start
  595.8 6.4 collective-permute-start
  604.4 6.4 collective-permute-start
  613.0 6.4 collective-permute-start
  621.6 6.4 collective-permute-start
  630.2 6.4 collective-permute-start
Sparse Core Ops, SparseCore 0:
  63.2 86.6 all-reduce.1
  558.5 17.8 all-gather.1
